TPU v7x, 32 devices: a whole 2x2x4 slice. The times are simulated.
32 devices in a mesh: expert: 8 (over z, y), blk: 4 (over x, core).
Axes of the slice: x: 2, y: 2, z: 4, core: 2. Of those that a mesh axis runs over, the one named last changes fastest.
Arguments:
- inputs: bfloat16 [8, 768, 1536], P('expert', 'blk'), may hold values from -6 to 6
- output_grads: bfloat16 [8, 768, 4096], P('expert', 'blk'), may hold values from -0.21875 to 0.21875
- route_counts: int32 [8, 4], P('expert', 'blk'), may hold values from 48 to 192, as said below
- left_rows: bfloat16 [8, 2304, 1536], P(None, 'expert', 'blk'), as said below
- left_lengths: int32 [8, 8], replicated, may hold values from 96 to 288, as said below
- right_inverse: bfloat16 [8, 4096, 4096], P('expert', 'blk'), may hold values from -0.09375 to 0.09375
Outputs:
- preconditioned: float32 [8, 4096, 1536], P('expert', 'blk')
Inputs may be any that keep to these rules, and one draw needn't show every extreme that they name: `route_counts`: for every expert, one device of blk holds exactly 192 routed tokens and one holds exactly 48. `left_lengths`: each row sums to 1536; in each row one owner holds exactly 288 rows and one exactly 96. `left_rows`: slots i * 288 + j with j >= left_lengths[e, i] are zero.
All inputs are finite; a program needn't handle non-finite values.
Results may differ from a plain program's by a relative error of at most 0.0041.
Values may be sent and summed in bfloat16 or wider, within the bound.
A program may use at most 128 MiB of HBM per device.

v0:
```python
import jax
import jax.numpy as jnp
from jax import lax
from jax.sharding import PartitionSpec as P


def shards(inputs, output_grads, route_counts, left_rows, left_lengths, right_inverse):
    token_rows = inputs[0]
    slot_count, width_in = token_rows.shape
    owners, piece_slots = (left_lengths.shape[1], left_rows.shape[1])
    live_rows = lax.broadcasted_iota(jnp.int32, (slot_count, 1), 0) < route_counts[0, 0]
    masked = jnp.where(live_rows, token_rows, jnp.zeros_like(token_rows))
    tokens = lax.all_gather(masked, "blk", axis=0, tiled=True)
    grads = lax.all_gather(output_grads[0], "blk", axis=0, tiled=True)
    arrived = lax.all_to_all(left_rows, "expert", split_axis=0, concat_axis=1, tiled=True)[0]
    lengths = lax.dynamic_index_in_dim(left_lengths, lax.axis_index("expert"), 0, keepdims=False)
    starts = jnp.cumsum(lengths) - lengths
    offset = lax.broadcasted_iota(jnp.int32, (owners, piece_slots), 1)
    row_index = jnp.where(offset < lengths[:, None], starts[:, None] + offset, -1)
    row_index = row_index.reshape(1, owners * piece_slots)
    select = lax.broadcasted_iota(jnp.int32, (width_in, 1), 0) == row_index
    picked = jnp.dot(tokens, select.astype(jnp.bfloat16), preferred_element_type=jnp.float32)
    picked = picked.astype(jnp.bfloat16)
    mixed = lax.dot_general(
        arrived, picked, (((0,), (1,)), ((), ())), preferred_element_type=jnp.float32
    ).astype(jnp.bfloat16)
    mixed = lax.all_gather(mixed, "blk", axis=0, tiled=True)
    trans_b = (((1,), (1,)), ((), ()))
    scores = lax.dot_general(
        right_inverse[0], grads, trans_b, preferred_element_type=jnp.float32
    ).astype(jnp.bfloat16)
    result = lax.dot_general(scores, mixed, trans_b, preferred_element_type=jnp.float32)
    return result[None]


def solution(mesh):
    in_specs = (
        P("expert", "blk", None),
        P("expert", "blk", None),
        P("expert", "blk"),
        P(None, "expert", "blk"),
        P(),
        P("expert", "blk", None),
    )
    out_specs = P("expert", "blk", None)
    return jax.shard_map(shards, mesh=mesh, in_specs=in_specs, out_specs=out_specs, check_vma=False)
```

profile of v0, /device:TPU:0, one launch (start us, length us, event | category | flops | bytes accessed | tf_op | source)
XLA Modules:
  0.0 165.5 jit_solution(11271811725548098723)
XLA Ops:
  6.5 0.0 all-gather.5.cloned.1.call-start
  7.2 2.0 %bitcast_select_fusion = bf16[192,1536]{1,0:T(8,128)(2,1)} fusion(bf16[1,192,1536]{2,1,0:T(8,128)(2,1)} %param.6, pred[192]{0:T(512)(128)(4,1)S(1)} %iota_compare_fusion.7), kind=kLoop, calls=%fused_computation.11 | loop fusion | flops 294912 | bytes 1179840 | tf_op jit(solution)/shard_map/jit(_where)/select_n | solution.py:12
  9.2 0.0 all-gather.5.cloned.1.call-update
  9.2 7.3 %all-to-all-start = ((bf16[8,288,384]{2,1,0:T(8,128)(2,1)}), bf16[8,288,384]{2,1,0:T(8,128)(2,1)S(1)}, u32[]{:S(2)}, u32[]{:S(2)}) async-start(bf16[8,288,384]{2,1,0:T(8,128)(2,1)} %param.9), calls=%async_computation | async-start | bytes 3538944 | tf_op jit(solution)/shard_map/all_to_all | solution.py:15
  16.5 0.0 all-gather.7.cloned.1.call-start
  16.6 0.7 fusion.16
  17.3 0.2 reduce-window.8
  17.5 0.7 bitcast_subtract_fusion
  18.2 0.1 add_select_fusion
  18.2 0.1 select_n.22
  18.3 39.4 %all-to-all-done = bf16[8,288,384]{2,1,0:T(8,128)(2,1)S(1)} async-done(((bf16[8,288,384]{2,1,0:T(8,128)(2,1)}), bf16[8,288,384]{2,1,0:T(8,128)(2,1)S(1)}, u32[]{:S(2)}, u32[]{:S(2)}) %all-to-all-start) | async-done | bytes 1769504 | tf_op jit(solution)/shard_map/all_to_all | solution.py:15
  57.8 0.0 all-gather.5.cloned.1.call-done
  57.8 10.0 %fusion.15 = bf16[384,768]{0,1:T(8,128)(2,1)} fusion(bf16[2304,384]{1,0:T(8,128)(2,1)S(1)} %bitcast.33, bf16[768,1536]{1,0:T(8,128)(2,1)} %all-gather.5.cloned.1.call-done, s32[2304]{0:T(1024)S(1)} %select_n.22), kind=kOutput, calls=%fused_computation.10 | convolution fusion | flops 6800375808 | bytes 4727808 | tf_op jit(solution)/shard_map/dot_general | solution.py:24
  67.8 0.0 all-gather.7.cloned.1.call-update
  67.8 0.0 all-gather.9.cloned.1.call-start
  67.8 0.7 all-gather.9.cloned.1.call-update
  68.5 22.5 %all-gather.7.cloned.1.call-done = bf16[1536,768]{0,1:T(8,128)(2,1)} async-done(((bf16[384,768]{0,1:T(8,128)(2,1)}), bf16[1536,768]{0,1:T(8,128)(2,1)}) %all-gather.7.cloned.1.call-update) | async-done | bytes 2359312 | tf_op jit(solution)/shard_map/all_gather | solution.py:27
  91.0 48.0 %all-gather.9.cloned.1.call-done = bf16[1,768,4096]{2,1,0:T(8,128)(2,1)} async-done(((bf16[1,192,4096]{2,1,0:T(8,128)(2,1)}), bf16[1,768,4096]{2,1,0:T(8,128)(2,1)}) %all-gather.9.cloned.1.call-update) | async-done | bytes 6291472 | tf_op jit(solution)/shard_map/all_gather | solution.py:14
  139.0 20.0 %convolution_bitcast_fusion = f32[1,1024,1536]{2,1,0:T(8,128)} fusion(bf16[1536,768]{0,1:T(8,128)(2,1)} %all-gather.7.cloned.1.call-done, bf16[1,768,4096]{2,1,0:T(8,128)(2,1)} %all-gather.9.cloned.1.call-done, bf16[1,1024,4096]{2,1,0:T(8,128)(2,1)} %param.11), kind=kOutput, calls=%fused_computation.7 | convolution fusion | flops 8859156480 | bytes 23330816 | tf_op jit(solution)/shard_map/dot_general | solution.py:32
  (1 shorter events, 0.0 us)
Async XLA Ops:
  6.5 51.2 %all-gather.5.cloned.1.call-start = ((), (), s32[]{:S(2)}) async-start(), calls=%async_computation.1 | async-start | bytes 2949120 | tf_op jit(solution)/shard_map/all_gather | solution.py:13
  9.2 48.5 %all-to-all-start = ((bf16[8,288,384]{2,1,0:T(8,128)(2,1)}), bf16[8,288,384]{2,1,0:T(8,128)(2,1)S(1)}, u32[]{:S(2)}, u32[]{:S(2)}) async-start(bf16[8,288,384]{2,1,0:T(8,128)(2,1)} %param.9), calls=%async_computation | async-start | bytes 3538944 | tf_op jit(solution)/shard_map/all_to_all | solution.py:15
  16.5 74.5 %all-gather.7.cloned.1.call-start = ((), (), s32[]{:S(2)}) async-start(), calls=%async_computation.2 | async-start | bytes 2949120 | tf_op jit(solution)/shard_map/all_gather | solution.py:27
  67.8 71.2 %all-gather.9.cloned.1.call-start = ((), (), s32[]{:S(2)}) async-start(), calls=%async_computation.3 | async-start | bytes 7864320 | tf_op jit(solution)/shard_map/all_gather | solution.py:14
Sparse Core Ops, SparseCore 0:
  9.3 26.7 all-gather.4
  67.9 23.0 all-gather.6
  92.6 46.3 all-gather.8
where the time goes:
time: 166 us
  waiting for transfers between devices  111 us (67%)
  matrix products  30 us (18%)
  between operations  13.8 us (8%)
  starting transfers between devices  7.4 us (4%)
  other arithmetic  2.95 us (2%)
    all_gather x1, waiting for transfers between devices, shards(): grads = lax.all_gather(output_grads[0], 'blk', axis=0, tiled=True)  48 us
    all_to_all x1, waiting for transfers between devices, shards(): lax.all_to_all(left_rows, 'expert', split_axis=0, concat_axis=1, tiled=True)  39.4 us
    all_gather x1, waiting for transfers between devices, shards(): mixed = lax.all_gather(mixed, 'blk', axis=0, tiled=True)  22.5 us
    dot_general x1, matrix products, shards(): lax.dot_general(scores, mixed, trans_b, preferred_element_type=jnp.float32)  20 us
    dot_general x1, matrix products, shards(): lax.dot_general(arrived, picked, (((0,), (1,)), ((), ())), preferred_elem...  10 us
    all_to_all x1, starting transfers between devices, shards(): lax.all_to_all(left_rows, 'expert', split_axis=0, concat_axis=1, tiled=True)  7.32 us
  transfers between devices with their start and end apart: 4, of which 3 were waited for; matrix products, arithmetic and copies ran while one was open for 1% of the time, Pallas kernels for 0%

commit v1 on v0

--- a/solution.py
+++ b/solution.py
@@ -2,6 +2,29 @@
 import jax.numpy as jnp
 from jax import lax
 from jax.sharding import PartitionSpec as P
+
+
+def laid_out(pieces, dim):
+    pieces = jnp.moveaxis(pieces, 0, dim)
+    shape = pieces.shape
+    return pieces.reshape(*shape[:dim], shape[dim] * shape[dim + 1], *shape[dim + 2 :])
+
+
+def collected_by_bits(array, axis):
+    peers, index = (lax.axis_size(axis), lax.axis_index(axis))
+    blocks, stride = (array[None], 1)
+    while stride < peers:
+        received = lax.ppermute(blocks, axis, [(i, i ^ stride) for i in range(peers)])
+        low = index & stride == 0
+        blocks = jnp.concatenate(
+            [jnp.where(low, blocks, received), jnp.where(low, received, blocks)]
+        )
+        stride *= 2
+    return blocks
+
+
+def collect(x, axis, dim):
+    return laid_out(collected_by_bits(x, axis), dim)
 
 
 def shards(inputs, output_grads, route_counts, left_rows, left_lengths, right_inverse):
@@ -11,7 +34,7 @@
     live_rows = lax.broadcasted_iota(jnp.int32, (slot_count, 1), 0) < route_counts[0, 0]
     masked = jnp.where(live_rows, token_rows, jnp.zeros_like(token_rows))
     tokens = lax.all_gather(masked, "blk", axis=0, tiled=True)
-    grads = lax.all_gather(output_grads[0], "blk", axis=0, tiled=True)
+    grads = collect(output_grads[0], "blk", 0)
     arrived = lax.all_to_all(left_rows, "expert", split_axis=0, concat_axis=1, tiled=True)[0]
     lengths = lax.dynamic_index_in_dim(left_lengths, lax.axis_index("expert"), 0, keepdims=False)
     starts = jnp.cumsum(lengths) - lengths

time: 166 us -> 143 us (0.86)
  waiting for transfers between devices: 111 us -> 80 us
  other arithmetic: 2.95 us -> 12.5 us
  matrix products: 30 us -> 26.5 us
    all_gather x1 -> x0, waiting for transfers between devices: 48 us -> none  [shards(): grads = lax.all_gather(output_grads[0], 'blk', axis=0, tiled=True)]
    ppermute x0 -> x2, waiting for transfers between devices: none -> 45.5 us  [collected_by_bits(): lax.ppermute(blocks, axis, [(i, i ^ stride) for i in range(peers)])]
    all_gather x1, waiting for transfers between devices: 22.5 us -> 0.01 us  [shards(): mixed = lax.all_gather(mixed, 'blk', axis=0, tiled=True)]
    concatenate x0 -> x2, other arithmetic: none -> 5.14 us  [collected_by_bits(): jnp.concatenate([jnp.where(low, blocks, received), jnp.where(low, receive...]
    all_to_all x1, waiting for transfers between devices: 39.4 us -> 34.4 us  [shards(): lax.all_to_all(left_rows, 'expert', split_axis=0, concat_axis=1, tiled=True)]
    select_n x0 -> x2, other arithmetic: none -> 4.45 us  [collected_by_bits(): jnp.where(low, blocks, received)]
    dot_general x1, matrix products: 20 us -> 15.9 us  [shards(): lax.dot_general(scores, mixed, trans_b, preferred_element_type=jnp.float32)]
    ppermute x0 -> x2, starting transfers between devices: none -> 2.04 us  [collected_by_bits(): lax.ppermute(blocks, axis, [(i, i ^ stride) for i in range(peers)])]
  transfers between devices with their start and end apart: 4 -> 5, of which waited for: 3 -> 2; matrix products, arithmetic and copies ran while one was open for 1% -> 15% of each run, Pallas kernels for 0% -> 0%
where the time goes in v1:
time: 143 us
  waiting for transfers between devices  80 us (56%)
  matrix products  26.5 us (19%)
  between operations  14.1 us (10%)
  other arithmetic  12.5 us (9%)
  starting transfers between devices  8.93 us (6%)
    ppermute x2, waiting for transfers between devices, collected_by_bits(): lax.ppermute(blocks, axis, [(i, i ^ stride) for i in range(peers)])  45.5 us
    all_to_all x1, waiting for transfers between devices, shards(): lax.all_to_all(left_rows, 'expert', split_axis=0, concat_axis=1, tiled=True)  34.4 us
    dot_general x1, matrix products, shards(): lax.dot_general(scores, mixed, trans_b, preferred_element_type=jnp.float32)  15.9 us
    dot_general x1, matrix products, shards(): lax.dot_general(arrived, picked, (((0,), (1,)), ((), ())), preferred_elem...  10.6 us
    all_to_all x1, starting transfers between devices, shards(): lax.all_to_all(left_rows, 'expert', split_axis=0, concat_axis=1, tiled=True)  6.85 us
    concatenate x2, other arithmetic, collected_by_bits(): jnp.concatenate([jnp.where(low, blocks, received), jnp.where(low, receive...  5.14 us
    select_n x2, other arithmetic, collected_by_bits(): jnp.where(low, blocks, received)  4.45 us
  transfers between devices with their start and end apart: 5, of which 2 were waited for; matrix products, arithmetic and copies ran while one was open for 15% of the time, Pallas kernels for 0%

profile of v1, /device:TPU:0, one launch (start us, length us, event | category | flops | bytes accessed | tf_op | source)
XLA Modules:
  0.0 142.8 jit_solution(7676264290474321004)
XLA Ops:
  6.5 0.0 all-gather.3.cloned.1.call-start
  7.2 2.0 %bitcast_select_fusion = bf16[192,1536]{1,0:T(8,128)(2,1)} fusion(bf16[1,192,1536]{2,1,0:T(8,128)(2,1)} %param.6, pred[192]{0:T(512)(128)(4,1)S(1)} %iota_compare_fusion.7), kind=kLoop, calls=%fused_computation.16 | loop fusion | flops 294912 | bytes 1179840 | tf_op jit(solution)/shard_map/jit(_where)/select_n | solution.py:35
  9.2 0.0 all-gather.3.cloned.1.call-update
  9.2 0.6 collective-permute-start
  9.8 6.8 %all-to-all-start = ((bf16[8,288,384]{2,1,0:T(8,128)(2,1)}), bf16[8,288,384]{2,1,0:T(8,128)(2,1)}, u32[]{:S(2)}, u32[]{:S(2)}) async-start(bf16[8,288,384]{2,1,0:T(8,128)(2,1)} %param.9), calls=%async_computation | async-start | bytes 3538944 | tf_op jit(solution)/shard_map/all_to_all | solution.py:38
  16.6 0.0 all-gather.5.cloned.1.call-start
  16.7 0.7 fusion.11
  17.4 0.2 reduce-window.8
  17.6 0.7 bitcast_subtract_fusion
  18.3 0.1 add_select_fusion
  18.3 0.1 select_n.52
  18.4 0.0 collective-permute-done
  18.4 2.3 %broadcast_select_fusion.3 = (bf16[1,192,4096]{2,1,0:T(8,128)(2,1)S(1)}, bf16[1,192,4096]{2,1,0:T(8,128)(2,1)S(1)}) fusion(bf16[1,192,4096]{2,1,0:T(8,128)(2,1)} %param.7, bf16[1,192,4096]{2,1,0:T(8,128)(2,1)} %collective-permute-done, pred[]{:T(512)S(6)} %eq.20), kind=kLoop, calls=%fused_computation.13 | loop fusion | flops 1572864 | bytes 6291457 | tf_op jit(solution)/shard_map/jit(_where)/select_n | solution.py:20
  20.8 1.9 %pad_maximum_fusion.1 = bf16[2,192,4096]{2,1,0:T(8,128)(2,1)} fusion(bf16[1,192,4096]{2,1,0:T(8,128)(2,1)S(1)} %get-tuple-element.10, bf16[1,192,4096]{2,1,0:T(8,128)(2,1)S(1)} %get-tuple-element.9), kind=kLoop, calls=%fused_computation.8 | loop fusion | flops 1572864 | bytes 6291456 | tf_op jit(solution)/shard_map/concatenate | solution.py:19
  22.7 1.5 %collective-permute-start.1 = (bf16[2,192,4096]{2,1,0:T(8,128)(2,1)}, bf16[2,192,4096]{2,1,0:T(8,128)(2,1)}, u32[]{:S(2)}, u32[]{:S(2)}) collective-permute-start(bf16[2,192,4096]{2,1,0:T(8,128)(2,1)} %pad_maximum_fusion.1), channel_id=1, source_target_pairs={{0,2},{1,3},{2,0},{3,1},{4,6},{5,7},{6,4},{7,5},{8,10},{9,11},{10,... | collective-permute-start | bytes 9437192 | tf_op jit(solution)/shard_map/ppermute | solution.py:17
  24.2 34.4 %all-to-all-done = bf16[8,288,384]{2,1,0:T(8,128)(2,1)} async-done(((bf16[8,288,384]{2,1,0:T(8,128)(2,1)}), bf16[8,288,384]{2,1,0:T(8,128)(2,1)}, u32[]{:S(2)}, u32[]{:S(2)}) %all-to-all-start) | async-done | bytes 1769504 | tf_op jit(solution)/shard_map/all_to_all | solution.py:38
  58.6 0.0 all-gather.3.cloned.1.call-done
  58.6 10.6 %fusion.8 = bf16[384,768]{0,1:T(8,128)(2,1)} fusion(bf16[2304,384]{1,0:T(8,128)(2,1)} %bitcast.7, bf16[768,1536]{1,0:T(8,128)(2,1)} %all-gather.3.cloned.1.call-done, s32[2304]{0:T(1024)S(1)} %select_n.52), kind=kOutput, calls=%fused_computation.15 | convolution fusion | flops 6800375808 | bytes 4727808 | tf_op jit(solution)/shard_map/dot_general | solution.py:47
  69.2 0.0 all-gather.5.cloned.1.call-update
  69.3 45.5 %collective-permute-done.1 = bf16[2,192,4096]{2,1,0:T(8,128)(2,1)} collective-permute-done((bf16[2,192,4096]{2,1,0:T(8,128)(2,1)}, bf16[2,192,4096]{2,1,0:T(8,128)(2,1)}, u32[]{:S(2)}, u32[]{:S(2)}) %collective-permute-start.1) | collective-permute-done | bytes 3145760 | tf_op jit(solution)/shard_map/ppermute | solution.py:17
  114.8 2.1 %broadcast_select_fusion.1 = (bf16[2,192,4096]{2,1,0:T(8,128)(2,1)S(1)}, bf16[2,192,4096]{2,1,0:T(8,128)(2,1)S(1)}) fusion(bf16[2,192,4096]{2,1,0:T(8,128)(2,1)} %collective-permute-done.1, pred[]{:T(512)S(6)} %eq.19, bf16[1,192,4096]{2,1,0:T(8,128)(2,1)S(1)} %get-tuple-element.10, bf16[1,192,4096]{2,1,0:T(8,128)(2,1)S(1)} %get-tuple-element.9), kind=kLoop, calls=%fused_computation.10 | loop fusion | flops 4718592 | bytes 12582913 | tf_op jit(solution)/shard_map/jit(_where)/select_n | solution.py:20
  116.9 3.2 %pad_maximum_fusion = bf16[4,192,4096]{2,1,0:T(8,128)(2,1)} fusion(bf16[2,192,4096]{2,1,0:T(8,128)(2,1)S(1)} %get-tuple-element.8, bf16[2,192,4096]{2,1,0:T(8,128)(2,1)S(1)} %get-tuple-element.7), kind=kLoop, calls=%fused_computation.5 | loop fusion | flops 3145728 | bytes 12582912 | tf_op jit(solution)/shard_map/concatenate | solution.py:19
  120.1 0.0 all-gather.5.cloned.1.call-done
  120.1 15.9 %convolution_bitcast_fusion = f32[1,1024,1536]{2,1,0:T(8,128)} fusion(bf16[1536,768]{0,1:T(8,128)(2,1)} %all-gather.5.cloned.1.call-done, bf16[768,4096]{1,0:T(8,128)(2,1)} %bitcast.28, bf16[1,1024,4096]{2,1,0:T(8,128)(2,1)} %param.11), kind=kOutput, calls=%fused_computation.7 | convolution fusion | flops 8859156480 | bytes 23330816 | tf_op jit(solution)/shard_map/dot_general | solution.py:55
  (1 shorter events, 0.0 us)
Async XLA Ops:
  6.5 52.1 %all-gather.3.cloned.1.call-start = ((), (), s32[]{:S(2)}) async-start(), calls=%async_computation.1 | async-start | bytes 2949120 | tf_op jit(solution)/shard_map/all_gather | solution.py:36
  9.2 9.2 %collective-permute-start = (bf16[1,192,4096]{2,1,0:T(8,128)(2,1)}, bf16[1,192,4096]{2,1,0:T(8,128)(2,1)}, u32[]{:S(2)}, u32[]{:S(2)}) collective-permute-start(bf16[1,192,4096]{2,1,0:T(8,128)(2,1)} %param.7), channel_id=1, source_target_pairs={{0,1},{1,0},{2,3},{3,2},{4,5},{5,4},{6,7},{7,6},{8,9},{9,8},{10,11... | collective-permute-start | bytes 4718600 | tf_op jit(solution)/shard_map/ppermute | solution.py:17
  9.8 48.8 %all-to-all-start = ((bf16[8,288,384]{2,1,0:T(8,128)(2,1)}), bf16[8,288,384]{2,1,0:T(8,128)(2,1)}, u32[]{:S(2)}, u32[]{:S(2)}) async-start(bf16[8,288,384]{2,1,0:T(8,128)(2,1)} %param.9), calls=%async_computation | async-start | bytes 3538944 | tf_op jit(solution)/shard_map/all_to_all | solution.py:38
  16.6 103.5 %all-gather.5.cloned.1.call-start = ((), (), s32[]{:S(2)}) async-start(), calls=%async_computation.2 | async-start | bytes 2949120 | tf_op jit(solution)/shard_map/all_gather | solution.py:50
  22.7 92.1 %collective-permute-start.1 = (bf16[2,192,4096]{2,1,0:T(8,128)(2,1)}, bf16[2,192,4096]{2,1,0:T(8,128)(2,1)}, u32[]{:S(2)}, u32[]{:S(2)}) collective-permute-start(bf16[2,192,4096]{2,1,0:T(8,128)(2,1)} %pad_maximum_fusion.1), channel_id=1, source_target_pairs={{0,2},{1,3},{2,0},{3,1},{4,6},{5,7},{6,4},{7,5},{8,10},{9,11},{10,... | collective-permute-start | bytes 9437192 | tf_op jit(solution)/shard_map/ppermute | solution.py:17
Sparse Core Ops, SparseCore 0:
  9.3 35.6 all-gather.2
  69.4 35.7 all-gather.4
